TPU v7x, 32 devices: a whole 2x2x4 slice. The times are simulated.
32 devices in a mesh: dp: 2 (over x), expert: 16 (over z, y, core).
Axes of the slice: x: 2, y: 2, z: 4, core: 2. Of those that a mesh axis runs over, the one named last changes fastest.
Arguments:
- saved_inputs: bfloat16 [1024, 3584], P('expert'), may hold values from -6 to 6
- output_grad: bfloat16 [1024, 3584], P('expert'), may hold values from -6 to 6
- routes: int32 [1024, 8], P('expert'), may hold values from 0 to 15, all different within a row; in each aligned block of 64 rows (0 to 63, 64 to 127, ...) at most 36 rows name the same one
- route_gates: bfloat16 [1024, 8], P('expert'), may hold values from 0.099609375 to 1
- expert_gate: bfloat16 [16, 3584, 1024], P('expert', None, 'dp'), may hold values from -0.09375 to 0.09375
- expert_up: bfloat16 [16, 3584, 1024], P('expert', None, 'dp'), may hold values from -0.09375 to 0.09375
- expert_down: bfloat16 [16, 1024, 3584], P('expert', 'dp'), may hold values from -0.1875 to 0.1875
- proj_basis: bfloat16 [16, 1024, 128], P('expert', 'dp'), may hold values from -0.1875 to 0.1875
Outputs:
- input_grad: bfloat16 [1024, 3584], P('expert', 'dp')
- projected: float32 [16, 3584, 3, 128], P('expert', 'dp')
Inputs may be any that keep to these rules, and one draw needn't show every extreme that they name: Within each aligned block of 64 tokens no expert is named by more than 36 routes, and in every draw some expert is named by exactly 36.
All inputs are finite; a program needn't handle non-finite values.
Results may differ from a plain program's by a relative error of at most 0.009.
Values may be sent and summed in bfloat16 or wider, within the bound.
A program may use at most 128 MiB of HBM per device.

v0:
```python
import jax
import jax.numpy as jnp
from jax import lax
from jax.sharding import PartitionSpec as P


def slot_form(
    saved_inputs, output_grad, routes, route_gates, expert_gate, expert_up, expert_down, proj_basis
):
    token_count, model_width = saved_inputs.shape
    top_count = routes.shape[1]
    expert_count = lax.axis_size("expert")
    group_count = lax.axis_size("dp")
    capacity = token_count * top_count * 9 // (8 * expert_count)
    slot_count = expert_count * capacity
    column_width = model_width // group_count
    route_count = token_count * top_count
    flat_routes = routes.reshape(-1)
    one_hot = (flat_routes[:, None] == jnp.arange(expert_count, dtype=jnp.int32)[None, :]).astype(
        jnp.int32
    )
    earlier = jnp.sum((jnp.cumsum(one_hot, axis=0) - one_hot) * one_hot, axis=1)
    target_slot = flat_routes * capacity + earlier
    slot_owner = (
        jnp.full((slot_count,), route_count, jnp.int32)
        .at[target_slot]
        .set(jnp.arange(route_count, dtype=jnp.int32))
    )
    filled = slot_owner < route_count
    safe_route = jnp.minimum(slot_owner, route_count - 1)
    source_token = safe_route // top_count
    zero_half = jnp.zeros((), jnp.bfloat16)
    gate_slots = jnp.where(filled, route_gates.reshape(-1)[safe_route], zero_half).reshape(
        expert_count, capacity
    )
    token_map = (
        (source_token[None, :] == jnp.arange(token_count, dtype=jnp.int32)[:, None])
        & filled[None, :]
    ).astype(jnp.bfloat16)
    contract_first = (((0,), (0,)), ((), ()))

    def to_slots(source_rows):
        picked = lax.dot_general(
            token_map, source_rows, contract_first, preferred_element_type=jnp.float32
        ).astype(jnp.bfloat16)
        return picked.reshape(expert_count, capacity * source_rows.shape[1])

    recv_inputs, recv_grads, recv_gates = (
        lax.all_to_all(to_slots(saved_inputs), "expert", split_axis=0, concat_axis=0, tiled=True),
        lax.all_to_all(to_slots(output_grad), "expert", split_axis=0, concat_axis=0, tiled=True),
        lax.all_to_all(gate_slots, "expert", split_axis=0, concat_axis=0, tiled=True),
    )
    input_rows = recv_inputs.reshape(slot_count, model_width)
    grad_rows = recv_grads.reshape(slot_count, model_width)
    gain = recv_gates.reshape(slot_count, 1).astype(jnp.float32)
    gate_w = expert_gate[0]
    up_w = expert_up[0]
    down_w = expert_down[0]
    basis = proj_basis[0]
    rank_width = basis.shape[1]
    contract_last = (((1,), (1,)), ((), ()))
    pre_gate = jnp.dot(input_rows, gate_w, preferred_element_type=jnp.float32)
    pre_up = jnp.dot(input_rows, up_w, preferred_element_type=jnp.float32)
    grad_hidden = lax.dot_general(
        grad_rows, down_w, contract_last, preferred_element_type=jnp.float32
    )
    sigma = jax.nn.sigmoid(pre_gate)
    silu_val = pre_gate * sigma
    scaled = gain * grad_hidden
    grad_up = (scaled * silu_val).astype(jnp.bfloat16)
    grad_gate = (scaled * pre_up * sigma * (1.0 + pre_gate * (1.0 - sigma))).astype(jnp.bfloat16)
    hidden = (silu_val * pre_up).astype(jnp.bfloat16)
    part_rows = (
        lax.dot_general(grad_gate, gate_w, contract_last, preferred_element_type=jnp.float32)
        + lax.dot_general(grad_up, up_w, contract_last, preferred_element_type=jnp.float32)
    ).astype(jnp.bfloat16)
    coef_gate = jnp.dot(grad_gate, basis, preferred_element_type=jnp.float32).astype(jnp.bfloat16)
    coef_up = jnp.dot(grad_up, basis, preferred_element_type=jnp.float32).astype(jnp.bfloat16)
    coef_down = (gain * jnp.dot(hidden, basis, preferred_element_type=jnp.float32)).astype(
        jnp.bfloat16
    )
    coef_pair = jnp.concatenate([coef_gate, coef_up], axis=1)
    front = lax.dot_general(
        input_rows, coef_pair, contract_first, preferred_element_type=jnp.float32
    )
    rear = lax.dot_general(grad_rows, coef_down, contract_first, preferred_element_type=jnp.float32)
    summed_terms = lax.psum_scatter(
        jnp.concatenate([front, rear], axis=1).astype(jnp.bfloat16),
        "dp",
        scatter_dimension=0,
        tiled=True,
    ).astype(jnp.float32)
    projected = summed_terms.reshape(1, column_width, 3, rank_width)
    returned = lax.all_to_all(
        part_rows.reshape(expert_count, capacity * model_width),
        "expert",
        split_axis=0,
        concat_axis=0,
        tiled=True,
    )
    spread = jnp.dot(
        token_map, returned.reshape(slot_count, model_width), preferred_element_type=jnp.float32
    )
    token_grad = lax.psum_scatter(
        spread.astype(jnp.bfloat16), "dp", scatter_dimension=1, tiled=True
    )
    return (token_grad, projected)


def dense_form(
    saved_inputs, output_grad, routes, route_gates, expert_gate, expert_up, expert_down, proj_basis
):
    model_width = saved_inputs.shape[1]
    expert_count = lax.axis_size("expert")
    group_count = lax.axis_size("dp")
    column_width = model_width // group_count
    experts = jnp.arange(expert_count, dtype=jnp.int32)
    chosen = routes[:, :, None] == experts[None, None, :]
    gate_table = jnp.sum(
        jnp.where(chosen, route_gates.astype(jnp.float32)[:, :, None], 0.0), axis=1
    ).astype(jnp.bfloat16)
    all_gates = lax.all_gather(gate_table, "expert", axis=0, tiled=True)
    input_rows = lax.all_gather(saved_inputs, "expert", axis=0, tiled=True)
    grad_rows = lax.all_gather(output_grad, "expert", axis=0, tiled=True)
    own = experts == lax.axis_index("expert")
    gain = jnp.sum(
        jnp.where(own[None, :], all_gates.astype(jnp.float32), 0.0), axis=1, keepdims=True
    )
    gate_w = expert_gate[0]
    up_w = expert_up[0]
    down_w = expert_down[0]
    basis = proj_basis[0]
    rank_width = basis.shape[1]
    contract_first = (((0,), (0,)), ((), ()))
    contract_last = (((1,), (1,)), ((), ()))
    pre_gate = jnp.dot(input_rows, gate_w, preferred_element_type=jnp.float32)
    pre_up = jnp.dot(input_rows, up_w, preferred_element_type=jnp.float32)
    grad_hidden = lax.dot_general(
        grad_rows, down_w, contract_last, preferred_element_type=jnp.float32
    )
    sigma = jax.nn.sigmoid(pre_gate)
    silu_val = pre_gate * sigma
    scaled = gain * grad_hidden
    grad_up = (scaled * silu_val).astype(jnp.bfloat16)
    grad_gate = (scaled * pre_up * sigma * (1.0 + pre_gate * (1.0 - sigma))).astype(jnp.bfloat16)
    hidden = (silu_val * pre_up).astype(jnp.bfloat16)
    part_rows = (
        lax.dot_general(grad_gate, gate_w, contract_last, preferred_element_type=jnp.float32)
        + lax.dot_general(grad_up, up_w, contract_last, preferred_element_type=jnp.float32)
    ).astype(jnp.bfloat16)
    own_rows = lax.psum_scatter(part_rows, "expert", scatter_dimension=0, tiled=True)
    token_grad = lax.psum_scatter(own_rows, "dp", scatter_dimension=1, tiled=True)
    coef_gate = jnp.dot(grad_gate, basis, preferred_element_type=jnp.float32).astype(jnp.bfloat16)
    coef_up = jnp.dot(grad_up, basis, preferred_element_type=jnp.float32).astype(jnp.bfloat16)
    coef_down = (gain * jnp.dot(hidden, basis, preferred_element_type=jnp.float32)).astype(
        jnp.bfloat16
    )
    coef_pair = jnp.concatenate([coef_gate, coef_up], axis=1)
    front = lax.dot_general(
        input_rows, coef_pair, contract_first, preferred_element_type=jnp.float32
    )
    rear = lax.dot_general(grad_rows, coef_down, contract_first, preferred_element_type=jnp.float32)
    summed_terms = lax.psum_scatter(
        jnp.concatenate([front, rear], axis=1).astype(jnp.bfloat16),
        "dp",
        scatter_dimension=0,
        tiled=True,
    ).astype(jnp.float32)
    projected = summed_terms.reshape(1, column_width, 3, rank_width)
    return (token_grad, projected)


def on_device(*arrays):
    if lax.axis_size("expert") <= 2 * arrays[2].shape[1]:
        return dense_form(*arrays)
    return slot_form(*arrays)


def solution(mesh):
    placed = (
        P("expert", None),
        P("expert", None),
        P("expert", None),
        P("expert", None),
        P("expert", None, "dp"),
        P("expert", None, "dp"),
        P("expert", "dp", None),
        P("expert", "dp", None),
    )
    return jax.shard_map(
        on_device,
        mesh=mesh,
        in_specs=placed,
        out_specs=(P("expert", "dp"), P("expert", "dp", None, None)),
        check_vma=False,
    )
```

profile of v0, /device:TPU:0, one launch (start us, length us, event | category | flops | bytes accessed | tf_op | source)
XLA Modules:
  0.0 331.8 jit_solution(12688891040194044894)
XLA Ops:
  7.2 0.7 all-gather.6.cloned.1.call-update
  8.0 0.7 all-gather.4.cloned.1.call-update
  8.7 0.7 convert_element_type.32
  9.4 0.7 select_reduce_fusion.1
  10.1 23.8 %all-gather = bf16[16,64,16]{1,2,0:T(8,128)(2,1)S(1)} all-gather(bf16[1,64,16]{1,2,0:T(8,128)(2,1)S(1)} %bitcast.44), channel_id=1, replica_groups=mesh['dp'=2,'expert'=16] {'expert'}, dimensions={0}, use_global_device_ids=true | all-gather | bytes 34816 | tf_op jit(solution)/shard_map/all_gather | solution.py:122
  33.9 0.1 reshape.23
  34.1 0.1 select_reduce_fusion
  34.1 46.7 %all-gather.6.cloned.1.call-done = bf16[1024,3584]{1,0:T(8,128)(2,1)} async-done(((bf16[64,3584]{1,0:T(8,128)(2,1)}), bf16[1024,3584]{1,0:T(8,128)(2,1)}) %all-gather.6.cloned.1.call-update) | async-done | bytes 7340048 | tf_op jit(solution)/shard_map/all_gather | solution.py:123
  80.8 9.5 %fusion.4 = f32[1024,512]{1,0:T(8,128)} fusion(bf16[1024,3584]{1,0:T(8,128)(2,1)} %all-gather.6.cloned.1.call-done, bf16[1,3584,512]{2,1,0:T(8,128)(2,1)} %param.12), kind=kOutput, calls=%fused_computation.7 | convolution fusion | flops 3758096384 | bytes 13107200 | tf_op jit(solution)/shard_map/dot_general | solution.py:136
  90.4 5.3 %fusion.7 = f32[1024,512]{1,0:T(8,128)} fusion(bf16[1024,3584]{1,0:T(8,128)(2,1)S(1)} %copy-done.1, bf16[1,3584,512]{2,1,0:T(8,128)(2,1)S(1)} %copy-done.3), kind=kOutput, calls=%fused_computation.10 | convolution fusion | flops 3758096384 | bytes 13107200 | tf_op jit(solution)/shard_map/dot_general | solution.py:137
  95.6 53.9 %all-gather.4.cloned.1.call-done = bf16[1024,3584]{1,0:T(8,128)(2,1)} async-done(((bf16[64,3584]{1,0:T(8,128)(2,1)}), bf16[1024,3584]{1,0:T(8,128)(2,1)}) %all-gather.4.cloned.1.call-update) | async-done | bytes 7340048 | tf_op jit(solution)/shard_map/all_gather | solution.py:124
  149.5 10.2 %multiply_convert_fusion.1 = (bf16[1024,512]{1,0:T(8,128)(2,1)S(1)}, bf16[1024,512]{1,0:T(8,128)(2,1)S(1)}) fusion(f32[1024]{0:T(1024)S(1)} %select_reduce_fusion, f32[1024,512]{1,0:T(8,128)} %fusion.4, f32[1024,512]{1,0:T(8,128)} %fusion.7, bf16[1024,3584]{1,0:T(8,128)(2,1)} %all-gather.4.cloned.1.call-done, bf16[1,512,3584]{2,1,0:T(8,128)(2,1)} %param.14), kind=kOutput, calls=%fused_computation.16 | convolution fusion | flops 3765436416 | bytes 17305600 | tf_op jit(solution)/shard_map/dot_general | solution.py:138
  159.7 7.4 %fusion.2 = f32[1024,3584]{1,0:T(8,128)} fusion(bf16[1024,512]{1,0:T(8,128)(2,1)S(1)} %get-tuple-element.11, bf16[1,3584,512]{2,1,0:T(8,128)(2,1)S(1)} %copy-done.2), kind=kOutput, calls=%fused_computation.5 | convolution fusion | flops 3758096384 | bytes 19398656 | tf_op jit(solution)/shard_map/dot_general | solution.py:148
  167.2 9.4 %add_convert_fusion = bf16[1024,3584]{1,0:T(8,128)(2,1)} fusion(f32[1024,3584]{1,0:T(8,128)} %fusion.2, bf16[1024,512]{1,0:T(8,128)(2,1)S(1)} %get-tuple-element.10, bf16[1,3584,512]{2,1,0:T(8,128)(2,1)S(1)} %copy-done.4), kind=kOutput, calls=%fused_computation | convolution fusion | flops 3765436416 | bytes 26738688 | tf_op jit(solution)/shard_map/dot_general | solution.py:149
  176.6 0.2 reduce-scatter.8.cloned.1.call-start
  176.8 0.5 convolution_convert_fusion.2
  177.3 0.5 convolution_convert_fusion.3
  177.8 5.2 %fusion = bf16[3584,256]{0,1:T(8,128)(2,1)S(1)} fusion(bf16[1024,3584]{1,0:T(8,128)(2,1)} %all-gather.6.cloned.1.call-done, bf16[1024,128]{0,1:T(8,128)(2,1)S(1)} %convolution_convert_fusion.2, bf16[1024,128]{0,1:T(8,128)(2,1)S(1)} %convolution_convert_fusion.3), kind=kOutput, calls=%fused_computation.2 | convolution fusion | flops 1881014272 | bytes 9699328 | tf_op jit(solution)/shard_map/dot_general | solution.py:159
  182.9 7.3 %fusion.1 = bf16[3584,128]{0,1:T(8,128)(2,1)S(1)} fusion(bf16[1024,3584]{1,0:T(8,128)(2,1)} %all-gather.4.cloned.1.call-done, f32[1024,512]{1,0:T(8,128)} %fusion.7, f32[1024,512]{1,0:T(8,128)} %fusion.4, f32[1024]{0:T(1024)S(1)} %select_reduce_fusion, bf16[1,512,128]{2,1,0:T(8,128)(2,1)S(1)} %copy-done), kind=kOutput, calls=%fused_computation.4 | convolution fusion | flops 1077608448 | bytes 12587008 | tf_op jit(solution)/shard_map/dot_general | solution.py:162
  190.3 1.7 pad_maximum_fusion
  192.1 75.0 %reduce-scatter.4.cloned.1.call-done = bf16[64,3584]{1,0:T(8,128)(2,1)} async-done(((bf16[1024,3584]{1,0:T(8,128)(2,1)}), bf16[64,3584]{1,0:T(8,128)(2,1)}) %reduce-scatter.4.cloned.1.call-update) | async-done | bytes 458768 | tf_op jit(solution)/shard_map/reduce_scatter | solution.py:151
  267.1 41.6 %reduce-scatter.8.cloned.1.call-done = bf16[1792,384]{0,1:T(8,128)(2,1)} async-done(((bf16[3584,384]{0,1:T(8,128)(2,1)}), bf16[1792,384]{0,1:T(8,128)(2,1)}) %reduce-scatter.8.cloned.1.call-update) | async-done | bytes 1376272 | tf_op jit(solution)/shard_map/reduce_scatter | solution.py:163
  308.7 2.9 copy.21
  311.6 13.7 %reduce-scatter.6.cloned.1.call-done = bf16[64,1792]{1,0:T(8,128)(2,1)} async-done(((bf16[64,3584]{1,0:T(8,128)(2,1)}), bf16[64,1792]{1,0:T(8,128)(2,1)}) %reduce-scatter.6.cloned.1.call-update) | async-done | bytes 229392 | tf_op jit(solution)/shard_map/reduce_scatter | solution.py:152
  (19 shorter events, 0.3 us)
Async XLA Ops:
  7.2 169.6 %copy-start = (bf16[1,512,128]{2,1,0:T(8,128)(2,1)S(1)}, bf16[1,512,128]{2,1,0:T(8,128)(2,1)}, u32[]{:S(2)}) copy-start(bf16[1,512,128]{2,1,0:T(8,128)(2,1)} %param.15) | copy-start | bytes 393220
  7.2 73.6 %all-gather.6.cloned.1.call-start = ((), (), s32[]{:S(2)}) async-start(), calls=%async_computation.4 | async-start | bytes 7798784 | tf_op jit(solution)/shard_map/all_gather | solution.py:123
  7.9 141.6 %all-gather.4.cloned.1.call-start = ((), (), s32[]{:S(2)}) async-start(), calls=%async_computation.3 | async-start | bytes 7798784 | tf_op jit(solution)/shard_map/all_gather | solution.py:124
  8.7 258.4 %reduce-scatter.4.cloned.1.call-start = ((), (), s32[]{:S(2)}) async-start(), calls=%async_computation.5 | async-start | bytes 7798784 | tf_op jit(solution)/shard_map/reduce_scatter | solution.py:151
  80.8 9.5 %copy-start.1 = (bf16[1024,3584]{1,0:T(8,128)(2,1)S(1)}, bf16[1024,3584]{1,0:T(8,128)(2,1)}, u32[]{:S(2)}) copy-start(bf16[1024,3584]{1,0:T(8,128)(2,1)} %all-gather.6.cloned.1.call-done) | copy-start | bytes 22020100
  80.8 9.5 %copy-start.3 = (bf16[1,3584,512]{2,1,0:T(8,128)(2,1)S(1)}, bf16[1,3584,512]{2,1,0:T(8,128)(2,1)}, u32[]{:S(2)}) copy-start(bf16[1,3584,512]{2,1,0:T(8,128)(2,1)} %param.13) | copy-start | bytes 11010052
  149.5 10.2 %copy-start.2 = (bf16[1,3584,512]{2,1,0:T(8,128)(2,1)S(1)}, bf16[1,3584,512]{2,1,0:T(8,128)(2,1)}, u32[]{:S(2)}) copy-start(bf16[1,3584,512]{2,1,0:T(8,128)(2,1)} %param.12) | copy-start | bytes 11010052
  159.7 7.4 %copy-start.4 = (bf16[1,3584,512]{2,1,0:T(8,128)(2,1)S(1)}, bf16[1,3584,512]{2,1,0:T(8,128)(2,1)}, u32[]{:S(2)}) copy-start(bf16[1,3584,512]{2,1,0:T(8,128)(2,1)} %param.13) | copy-start | bytes 11010052
  176.6 132.1 %reduce-scatter.8.cloned.1.call-start = ((), (), s32[]{:S(2)}) async-start(), calls=%async_computation.7 | async-start | bytes 4128768 | tf_op jit(solution)/shard_map/reduce_scatter | solution.py:163
  192.0 133.3 %reduce-scatter.6.cloned.1.call-start = ((), (), s32[]{:S(2)}) async-start(), calls=%async_computation.6 | async-start | bytes 688128 | tf_op jit(solution)/shard_map/reduce_scatter | solution.py:152
Sparse Core Ops, SparseCore 0:
  10.3 70.4 all-gather.5
  83.1 66.4 all-gather.3
  176.7 90.3 reduce-scatter.3
  269.8 38.8 reduce-scatter.7
  311.4 13.9 reduce-scatter.5
where the time goes:
time: 332 us
  waiting for transfers between devices  232 us (70%)
  matrix products  55.2 us (17%)
  blocking collectives  23.8 us (7%)
  between operations  13.9 us (4%)
    reduce_scatter x1, waiting for transfers between devices, dense_form(): lax.psum_scatter(part_rows, 'expert', scatter_dimension=0, tiled=True)  75 us
    all_gather x1, waiting for transfers between devices, dense_form(): grad_rows = lax.all_gather(output_grad, 'expert', axis=0, tiled=True)  53.9 us
    all_gather x1, waiting for transfers between devices, dense_form(): input_rows = lax.all_gather(saved_inputs, 'expert', axis=0, tiled=True)  46.7 us
    reduce_scatter x1, waiting for transfers between devices, dense_form(): lax.psum_scatter(jnp.concatenate([front, rear], axis=1).astype(jnp.bfloat...  41.6 us
    all_gather x1, blocking collectives, dense_form(): all_gates = lax.all_gather(gate_table, 'expert', axis=0, tiled=True)  23.8 us
    reduce_scatter x1, waiting for transfers between devices, dense_form(): lax.psum_scatter(own_rows, 'dp', scatter_dimension=1, tiled=True)  13.7 us
    dot_general x1, matrix products, dense_form(): lax.dot_general(grad_rows, down_w, contract_last, preferred_element_type=...  10.2 us
    dot_general x1, matrix products, dense_form(): pre_gate = jnp.dot(input_rows, gate_w, preferred_element_type=jnp.float32)  9.54 us
  transfers between devices with their start and end apart: 5, of which 5 were waited for; matrix products, arithmetic and copies ran while one was open for 10% of the time, Pallas kernels for 0%

commit v1 on v0

--- a/solution.py
+++ b/solution.py
@@ -120,7 +120,22 @@
         jnp.where(chosen, route_gates.astype(jnp.float32)[:, :, None], 0.0), axis=1
     ).astype(jnp.bfloat16)
     all_gates = lax.all_gather(gate_table, "expert", axis=0, tiled=True)
-    input_rows = lax.all_gather(saved_inputs, "expert", axis=0, tiled=True)
+    ready, even, e_next = (lax.psum(1, "expert"), lax.axis_index("expert"), saved_inputs.shape[0])
+    part_next, long_array = (saved_inputs, 1)
+    while long_array < ready:
+        part_next = jnp.concatenate(
+            [
+                part_next,
+                lax.ppermute(
+                    part_next,
+                    "expert",
+                    tuple(((u, (u - long_array) % ready) for u in range(ready))),
+                ),
+            ],
+            0,
+        )
+        long_array = 2 * long_array
+    input_rows = jnp.roll(part_next, even * e_next, 0)
     grad_rows = lax.all_gather(output_grad, "expert", axis=0, tiled=True)
     own = experts == lax.axis_index("expert")
     gain = jnp.sum(

time: 332 us -> 505 us (1.52)
  waiting for transfers between devices: 232 us -> 319 us
  blocking collectives: 23.8 us -> 97.3 us
  local copies, waits for them, and re-layouts: 3.04 us -> 11 us
  starting transfers between devices: 0.38 us -> 7.46 us
  matrix products: 55.2 us -> 50 us
    ppermute x0 -> x4, waiting for transfers between devices: none -> 173 us  [dense_form(): lax.ppermute(part_next, 'expert', tuple(((u, (u - long_array) % ready) fo...]
    all_gather x1, blocking collectives: 23.8 us -> 97.3 us  [dense_form(): all_gates = lax.all_gather(gate_table, 'expert', axis=0, tiled=True)]
    all_gather x1, waiting for transfers between devices: 53.9 us -> 0.01 us  [dense_form(): grad_rows = lax.all_gather(output_grad, 'expert', axis=0, tiled=True)]
    all_gather x1 -> x0, waiting for transfers between devices: 46.7 us -> none  [dense_form(): input_rows = lax.all_gather(saved_inputs, 'expert', axis=0, tiled=True)]
    reduce_scatter x1, waiting for transfers between devices: 75 us -> 89.4 us  [dense_form(): lax.psum_scatter(part_rows, 'expert', scatter_dimension=0, tiled=True)]
    ppermute x0 -> x4, starting transfers between devices: none -> 7.12 us  [dense_form(): lax.ppermute(part_next, 'expert', tuple(((u, (u - long_array) % ready) fo...]
    unnamed x11 -> x32, local copies, waits for them, and re-layouts: 2.93 us -> 8.5 us
  transfers between devices with their start and end apart: 5 -> 8, of which waited for: 5 -> 7; matrix products, arithmetic and copies ran while one was open for 10% -> 8% of each run, Pallas kernels for 0% -> 0%
where the time goes in v1:
time: 505 us
  waiting for transfers between devices  319 us (63%)
  blocking collectives  97.3 us (19%)
  matrix products  50 us (10%)
  between operations  14 us (3%)
  local copies, waits for them, and re-layouts  11 us (2%)
  starting transfers between devices  7.46 us (1%)
  other arithmetic  6.27 us (1%)
    ppermute x4, waiting for transfers between devices, dense_form(): lax.ppermute(part_next, 'expert', tuple(((u, (u - long_array) % ready) fo...  173 us
    all_gather x1, blocking collectives, dense_form(): all_gates = lax.all_gather(gate_table, 'expert', axis=0, tiled=True)  97.3 us
    reduce_scatter x1, waiting for transfers between devices, dense_form(): lax.psum_scatter(part_rows, 'expert', scatter_dimension=0, tiled=True)  89.4 us
    reduce_scatter x1, waiting for transfers between devices, dense_form(): lax.psum_scatter(jnp.concatenate([front, rear], axis=1).astype(jnp.bfloat...  41.7 us
    reduce_scatter x1, waiting for transfers between devices, dense_form(): lax.psum_scatter(own_rows, 'dp', scatter_dimension=1, tiled=True)  13.7 us
    dot_general x1, matrix products, dense_form(): lax.dot_general(grad_rows, down_w, contract_last, preferred_element_type=...  10.2 us
  transfers between devices with their start and end apart: 8, of which 7 were waited for; matrix products, arithmetic and copies ran while one was open for 8% of the time, Pallas kernels for 0%

profile of v1, /device:TPU:0, one launch (start us, length us, event | category | flops | bytes accessed | tf_op | source)
XLA Modules:
  0.0 504.9 jit_solution(10240183513865048776)
XLA Ops:
  8.0 5.5 %collective-permute-start = (bf16[64,3584]{1,0:T(8,128)(2,1)}, bf16[64,3584]{1,0:T(8,128)(2,1)S(1)}, u32[]{:S(2)}, u32[]{:S(2)}) collective-permute-start(bf16[64,3584]{1,0:T(8,128)(2,1)} %param.8), channel_id=1, source_target_pairs={{0,15},{1,0},{2,1},{3,2},{4,3},{5,4},{6,5},{7,6},{8,7},{9,8},{10,9... | collective-permute-start | bytes 1376264 | tf_op jit(solution)/shard_map/ppermute | solution.py:129
  13.5 6.3 %collective-permute-done = bf16[64,3584]{1,0:T(8,128)(2,1)S(1)} collective-permute-done((bf16[64,3584]{1,0:T(8,128)(2,1)}, bf16[64,3584]{1,0:T(8,128)(2,1)S(1)}, u32[]{:S(2)}, u32[]{:S(2)}) %collective-permute-start) | collective-permute-done | bytes 458784 | tf_op jit(solution)/shard_map/ppermute | solution.py:129
  19.8 1.3 pad_maximum_fusion.3
  21.7 33.4 %collective-permute-done.1 = bf16[128,3584]{1,0:T(8,128)(2,1)S(1)} collective-permute-done((bf16[128,3584]{1,0:T(8,128)(2,1)S(1)}, bf16[128,3584]{1,0:T(8,128)(2,1)S(1)}, u32[]{:S(2)}, u32[]{:S(2)}) %collective-permute-start.1) | collective-permute-done | bytes 917536 | tf_op jit(solution)/shard_map/ppermute | solution.py:129
  55.1 1.1 pad_maximum_fusion.2
  57.3 71.1 %collective-permute-done.2 = bf16[256,3584]{1,0:T(8,128)(2,1)S(1)} collective-permute-done((bf16[256,3584]{1,0:T(8,128)(2,1)S(1)}, bf16[256,3584]{1,0:T(8,128)(2,1)S(1)}, u32[]{:S(2)}, u32[]{:S(2)}) %collective-permute-start.2) | collective-permute-done | bytes 1835040 | tf_op jit(solution)/shard_map/ppermute | solution.py:129
  128.4 2.0 pad_maximum_fusion
  130.5 97.3 %all-gather = bf16[16,64,16]{1,2,0:T(8,128)(2,1)S(1)} all-gather(bf16[1,64,16]{1,2,0:T(8,128)(2,1)S(1)} %bitcast.39), channel_id=1, replica_groups=mesh['dp'=2,'expert'=16] {'expert'}, dimensions={0}, use_global_device_ids=true | all-gather | bytes 34816 | tf_op jit(solution)/shard_map/all_gather | solution.py:122
  229.3 62.5 %collective-permute-done.3 = bf16[512,3584]{1,0:T(8,128)(2,1)} collective-permute-done((bf16[512,3584]{1,0:T(8,128)(2,1)}, bf16[512,3584]{1,0:T(8,128)(2,1)}, u32[]{:S(2)}, u32[]{:S(2)}) %collective-permute-start.3) | collective-permute-done | bytes 3670048 | tf_op jit(solution)/shard_map/ppermute | solution.py:129
  291.8 2.3 constant_dynamic-update-slice_fusion.5
  294.3 2.4 constant_dynamic-update-slice_fusion
  297.5 5.8 %fusion.4 = f32[1024,512]{1,0:T(8,128)} fusion(bf16[2048,3584]{1,0:T(8,128)(2,1)S(1)} %constant_dynamic-update-slice_fusion, s32[]{:T(128)S(6)} %select_n.24, bf16[1,3584,512]{2,1,0:T(8,128)(2,1)S(1)} %copy-done.9), kind=kOutput, calls=%fused_computation.5 | convolution fusion | flops 3758096384 | bytes 13107204 | tf_op jit(solution)/shard_map/dot_general | solution.py:152
  303.2 1.1 copy-done.4
  304.3 5.3 %fusion.2 = f32[1024,512]{1,0:T(8,128)} fusion(bf16[2048,3584]{1,0:T(8,128)(2,1)S(1)} %constant_dynamic-update-slice_fusion, s32[]{:T(128)S(6)} %select_n.24, bf16[1,3584,512]{2,1,0:T(8,128)(2,1)S(1)} %copy-done.7), kind=kOutput, calls=%fused_computation.3 | convolution fusion | flops 3758096384 | bytes 13107204 | tf_op jit(solution)/shard_map/dot_general | solution.py:151
  309.6 10.2 %multiply_convert_fusion.1 = (bf16[1024,512]{1,0:T(8,128)(2,1)S(1)}, bf16[1024,512]{1,0:T(8,128)(2,1)S(1)}) fusion(f32[1024]{0:T(1024)S(1)} %select_reduce_fusion, f32[1024,512]{1,0:T(8,128)} %fusion.2, f32[1024,512]{1,0:T(8,128)} %fusion.4, bf16[1024,3584]{1,0:T(8,128)(2,1)} %all-gather.3.cloned.1.call-done, bf16[1,512,3584]{2,1,0:T(8,128)(2,1)} %param.14), kind=kOutput, calls=%fused_computation.20 | convolution fusion | flops 3765436416 | bytes 17305600 | tf_op jit(solution)/shard_map/dot_general | solution.py:153
  319.7 7.3 %fusion.10 = f32[1024,3584]{1,0:T(8,128)} fusion(bf16[1024,512]{1,0:T(8,128)(2,1)S(1)} %get-tuple-element.11, bf16[1,3584,512]{2,1,0:T(8,128)(2,1)S(1)} %copy-done.8), kind=kOutput, calls=%fused_computation.11 | convolution fusion | flops 3758096384 | bytes 19398656 | tf_op jit(solution)/shard_map/dot_general | solution.py:163
  327.0 9.2 %add_convert_fusion = bf16[1024,3584]{1,0:T(8,128)(2,1)} fusion(f32[1024,3584]{1,0:T(8,128)} %fusion.10, bf16[1024,512]{1,0:T(8,128)(2,1)S(1)} %get-tuple-element.10, bf16[1,3584,512]{2,1,0:T(8,128)(2,1)S(1)} %copy-done.10), kind=kOutput, calls=%fused_computation | convolution fusion | flops 3765436416 | bytes 26738688 | tf_op jit(solution)/shard_map/dot_general | solution.py:164
  337.4 5.1 %fusion.6 = bf16[3584,256]{0,1:T(8,128)(2,1)S(1)} fusion(bf16[2048,3584]{1,0:T(8,128)(2,1)} %copy-done.4, s32[]{:T(128)S(6)} %select_n.24, bf16[1024,128]{0,1:T(8,128)(2,1)S(1)} %convolution_convert_fusion.1, bf16[1024,128]{0,1:T(8,128)(2,1)S(1)} %convolution_convert_fusion.2), kind=kOutput, calls=%fused_computation.7 | convolution fusion | flops 1881014272 | bytes 9699332 | tf_op jit(solution)/shard_map/dot_general | solution.py:174
  342.6 6.3 %fusion.9 = bf16[3584,128]{0,1:T(8,128)(2,1)S(1)} fusion(bf16[1024,3584]{1,0:T(8,128)(2,1)} %all-gather.3.cloned.1.call-done, f32[1024,512]{1,0:T(8,128)} %fusion.4, f32[1024,512]{1,0:T(8,128)} %fusion.2, f32[1024]{0:T(1024)S(1)} %select_reduce_fusion, bf16[1,512,128]{2,1,0:T(8,128)(2,1)S(1)} %copy-done), kind=kOutput, calls=%fused_computation.9 | convolution fusion | flops 1077608448 | bytes 12587008 | tf_op jit(solution)/shard_map/dot_general | solution.py:177
  348.9 1.7 pad_maximum_fusion.1
  350.7 89.4 %reduce-scatter.4.cloned.1.call-done = bf16[64,3584]{1,0:T(8,128)(2,1)} async-done(((bf16[1024,3584]{1,0:T(8,128)(2,1)}), bf16[64,3584]{1,0:T(8,128)(2,1)}) %reduce-scatter.4.cloned.1.call-update) | async-done | bytes 458768 | tf_op jit(solution)/shard_map/reduce_scatter | solution.py:166
  440.1 41.7 %reduce-scatter.8.cloned.1.call-done = bf16[1792,384]{0,1:T(8,128)(2,1)} async-done(((bf16[3584,384]{0,1:T(8,128)(2,1)}), bf16[1792,384]{0,1:T(8,128)(2,1)}) %reduce-scatter.8.cloned.1.call-update) | async-done | bytes 1376272 | tf_op jit(solution)/shard_map/reduce_scatter | solution.py:178
  481.8 2.9 copy.21
  484.7 13.7 %reduce-scatter.6.cloned.1.call-done = bf16[64,1792]{1,0:T(8,128)(2,1)} async-done(((bf16[64,3584]{1,0:T(8,128)(2,1)}), bf16[64,1792]{1,0:T(8,128)(2,1)}) %reduce-scatter.6.cloned.1.call-update) | async-done | bytes 229392 | tf_op jit(solution)/shard_map/reduce_scatter | solution.py:167
  (49 shorter events, 6.1 us)
Async XLA Ops:
  7.2 329.3 %copy-start = (bf16[1,512,128]{2,1,0:T(8,128)(2,1)S(1)}, bf16[1,512,128]{2,1,0:T(8,128)(2,1)}, u32[]{:S(2)}) copy-start(bf16[1,512,128]{2,1,0:T(8,128)(2,1)} %param.15) | copy-start | bytes 393220
  7.2 121.2 %copy-start.1 = (bf16[64,3584]{1,0:T(8,128)(2,1)S(1)}, bf16[64,3584]{1,0:T(8,128)(2,1)}, u32[]{:S(2)}) copy-start(bf16[64,3584]{1,0:T(8,128)(2,1)} %param.8) | copy-start | bytes 1376260
  7.2 302.4 %all-gather.3.cloned.1.call-start = ((), (), s32[]{:S(2)}) async-start(), calls=%async_computation.3 | async-start | bytes 7798784 | tf_op jit(solution)/shard_map/all_gather | solution.py:139
  7.9 432.1 %reduce-scatter.4.cloned.1.call-start = ((), (), s32[]{:S(2)}) async-start(), calls=%async_computation.4 | async-start | bytes 7798784 | tf_op jit(solution)/shard_map/reduce_scatter | solution.py:166
  8.0 11.8 %collective-permute-start = (bf16[64,3584]{1,0:T(8,128)(2,1)}, bf16[64,3584]{1,0:T(8,128)(2,1)S(1)}, u32[]{:S(2)}, u32[]{:S(2)}) collective-permute-start(bf16[64,3584]{1,0:T(8,128)(2,1)} %param.8), channel_id=1, source_target_pairs={{0,15},{1,0},{2,1},{3,2},{4,3},{5,4},{6,5},{7,6},{8,7},{9,8},{10,9... | collective-permute-start | bytes 1376264 | tf_op jit(solution)/shard_map/ppermute | solution.py:129
  19.8 110.6 %copy-start.2 = (bf16[64,3584]{1,0:T(8,128)(2,1)}, bf16[64,3584]{1,0:T(8,128)(2,1)S(1)}, u32[]{:S(2)}) copy-start(bf16[64,3584]{1,0:T(8,128)(2,1)S(1)} %collective-permute-done) | copy-start | bytes 1376260
  21.1 34.0 %collective-permute-start.1 = (bf16[128,3584]{1,0:T(8,128)(2,1)S(1)}, bf16[128,3584]{1,0:T(8,128)(2,1)S(1)}, u32[]{:S(2)}, u32[]{:S(2)}) collective-permute-start(bf16[128,3584]{1,0:T(8,128)(2,1)S(1)} %pad_maximum_fusion.3), channel_id=1, source_target_pairs={{0,14},{1,15},{2,0},{3,1},{4,2},{5,3},{6,4},{7,5},{8,6},{9,7},{10,... | collective-permute-start | bytes 2752520 | tf_op jit(solution)/shard_map/ppermute | solution.py:129
  56.3 74.2 %copy-start.6 = (bf16[64,8]{0,1:T(8,128)(2,1)S(1)}, bf16[64,8]{0,1:T(8,128)(2,1)}, u32[]{:S(2)}) copy-start(bf16[64,8]{0,1:T(8,128)(2,1)} %param.11) | copy-start | bytes 3076
  56.3 74.2 %copy-start.5 = (s32[64,8]{0,1:T(8,128)S(1)}, s32[64,8]{0,1:T(8,128)}, u32[]{:S(2)}) copy-start(s32[64,8]{0,1:T(8,128)} %param.10) | copy-start | bytes 6148
  56.3 72.1 %collective-permute-start.2 = (bf16[256,3584]{1,0:T(8,128)(2,1)S(1)}, bf16[256,3584]{1,0:T(8,128)(2,1)S(1)}, u32[]{:S(2)}, u32[]{:S(2)}) collective-permute-start(bf16[256,3584]{1,0:T(8,128)(2,1)S(1)} %pad_maximum_fusion.2), channel_id=1, source_target_pairs={{0,12},{1,13},{2,14},{3,15},{4,0},{5,1},{6,2},{7,3},{8,4},{9,5},{1... | collective-permute-start | bytes 5505032 | tf_op jit(solution)/shard_map/ppermute | solution.py:129
  130.4 161.3 %collective-permute-start.3 = (bf16[512,3584]{1,0:T(8,128)(2,1)}, bf16[512,3584]{1,0:T(8,128)(2,1)}, u32[]{:S(2)}, u32[]{:S(2)}) collective-permute-start(bf16[512,3584]{1,0:T(8,128)(2,1)} %pad_maximum_fusion), channel_id=1, source_target_pairs={{0,8},{1,9},{2,10},{3,11},{4,12},{5,13},{6,14},{7,15},{8,0},{9,1},... | collective-permute-start | bytes 11010056 | tf_op jit(solution)/shard_map/ppermute | solution.py:129
  229.3 64.8 %copy-start.3 = (bf16[64,3584]{1,0:T(8,128)(2,1)S(1)}, bf16[64,3584]{1,0:T(8,128)(2,1)}, u32[]{:S(2)}) copy-start(bf16[64,3584]{1,0:T(8,128)(2,1)} %copy-done.2) | copy-start | bytes 1376260
  294.3 3.1 copy-start.9
  297.5 6.8 %copy-start.4 = (bf16[2048,3584]{1,0:T(8,128)(2,1)}, bf16[2048,3584]{1,0:T(8,128)(2,1)S(1)}, u32[]{:S(2)}) copy-start(bf16[2048,3584]{1,0:T(8,128)(2,1)S(1)} %constant_dynamic-update-slice_fusion) | copy-start | bytes 44040196
  297.5 6.8 %copy-start.7 = (bf16[1,3584,512]{2,1,0:T(8,128)(2,1)S(1)}, bf16[1,3584,512]{2,1,0:T(8,128)(2,1)}, u32[]{:S(2)}) copy-start(bf16[1,3584,512]{2,1,0:T(8,128)(2,1)} %param.12) | copy-start | bytes 11010052
  309.5 10.2 %copy-start.8 = (bf16[1,3584,512]{2,1,0:T(8,128)(2,1)S(1)}, bf16[1,3584,512]{2,1,0:T(8,128)(2,1)}, u32[]{:S(2)}) copy-start(bf16[1,3584,512]{2,1,0:T(8,128)(2,1)} %param.12) | copy-start | bytes 11010052
  319.7 7.3 %copy-start.10 = (bf16[1,3584,512]{2,1,0:T(8,128)(2,1)S(1)}, bf16[1,3584,512]{2,1,0:T(8,128)(2,1)}, u32[]{:S(2)}) copy-start(bf16[1,3584,512]{2,1,0:T(8,128)(2,1)} %param.13) | copy-start | bytes 11010052
  336.2 145.6 %reduce-scatter.8.cloned.1.call-start = ((), (), s32[]{:S(2)}) async-start(), calls=%async_computation.6 | async-start | bytes 4128768 | tf_op jit(solution)/shard_map/reduce_scatter | solution.py:178
  350.6 147.8 %reduce-scatter.6.cloned.1.call-start = ((), (), s32[]{:S(2)}) async-start(), calls=%async_computation.5 | async-start | bytes 688128 | tf_op jit(solution)/shard_map/reduce_scatter | solution.py:167
Sparse Core Ops, SparseCore 0:
  10.3 111.9 all-gather.2
  336.3 103.6 reduce-scatter.3
  442.9 38.8 reduce-scatter.7
  484.5 13.8 reduce-scatter.5
